TPU v7x, 128 devices: a whole 4x4x4 slice. The times are simulated.
128 devices in a mesh: tm: 8 (over y, x_hi), agent: 16 (over z, x_lo, core).
Axes of the slice: x: 4 (x_hi: 2, x_lo: 2; x = x_hi * 2 + x_lo), y: 4, z: 4, core: 2. Of those that a mesh axis runs over, the one named last changes fastest.
Arguments:
- tokens: bfloat16 [32, 1024, 1024], P('tm', 'agent'), may hold values from -6 to 6
- conv_taps: float32 [5, 1024], replicated, may hold values from -3 to 3
- norm_first: float32 [1024], replicated, may hold values from 0.1 to 1.9
- norm_second: float32 [1024], replicated, may hold values from 0.1 to 1.9
- norm_third: float32 [1024], replicated, may hold values from 0.1 to 1.9
- w_in: bfloat16 [1024, 3072], replicated, may hold values from -0.1875 to 0.1875
- w_out: bfloat16 [3072, 1024], replicated, may hold values from -0.109375 to 0.109375
- w_query: bfloat16 [1024, 1024], replicated, may hold values from -16 to 16
- w_key: bfloat16 [1024, 1024], replicated, may hold values from -16 to 16
- w_value: bfloat16 [1024, 1024], replicated, may hold values from -0.1875 to 0.1875
- w_output: bfloat16 [1024, 1024], replicated, may hold values from -0.1875 to 0.1875
- agent_order: int32 [1024], P('agent'), may hold values from 0 to 1023, each once
- present_steps: int32 [1024], P('agent'), may hold values from 1 to 32
Outputs:
- result: bfloat16 [32, 1024, 1024], P('tm', 'agent')
Inputs may be any that keep to these rules, and one draw needn't show every extreme that they name: `agent_order`: each of 0 to 1023 appears once.
All inputs are finite; a program needn't handle non-finite values.
Results may differ from a plain program's by a relative error of at most 0.012.
Values may be sent and summed in bfloat16 or wider, within the bound.
A program may use at most 192 MiB of HBM per device.

v0:
```python
import jax
import jax.numpy as jnp
from jax import lax
from jax.sharding import PartitionSpec as P

HEADS = 16
EPS = 1e-05


def shifted(shard, axis, by):
    count = lax.axis_size(axis)
    pairs = [(i, i + by) for i in range(count) if 0 <= i + by < count]
    return lax.ppermute(shard, axis, pairs)


def normed_rows(rows, gain):
    values = rows.astype(jnp.float32)
    scale = lax.rsqrt(jnp.mean(values * values, axis=-1, keepdims=True) + EPS)
    return values * scale * gain


def make_absorb(query, own_order, steps, heads_here, project):
    step_count, agent_count, width = query.shape
    head_size = width // heads_here
    scale = head_size ** (-0.5)
    split_query = query.reshape(step_count, agent_count, heads_here, head_size)
    init = (
        jnp.full((step_count, heads_here, agent_count), -1e30, jnp.float32),
        jnp.zeros((step_count, heads_here, agent_count), jnp.float32),
        jnp.zeros((step_count, agent_count, heads_here, head_size), jnp.float32),
    )

    def absorb(carry, piece, start):
        best, total, summed = carry
        key_piece, value_piece, order_piece, present_piece = project(piece)
        count = key_piece.shape[1]
        key_piece = key_piece.reshape(step_count, count, heads_here, head_size)
        value_piece = value_piece.reshape(step_count, count, heads_here, head_size)
        scores = (
            jnp.einsum(
                "sahd,sbhd->shab", split_query, key_piece, preferred_element_type=jnp.float32
            )
            * scale
        )
        other_order = order_piece[0]
        earlier = other_order[None, None, :] < own_order[None, :, None]
        alive = steps[:, None, None] < present_piece[0][None, None, :]
        itself = other_order[None, None, :] == own_order[None, :, None]
        visible = (earlier & alive | itself)[:, None]
        masked = jnp.where(visible, scores, -1e30)
        fresh = jnp.maximum(best, jnp.max(masked, axis=-1))
        weights = jnp.where(visible, jnp.exp(masked - fresh[..., None]), 0.0).astype(jnp.bfloat16)
        total = jnp.sum(weights.astype(jnp.float32), axis=-1)
        part_sum = jnp.einsum(
            "shab,sbhd->sahd", weights, value_piece, preferred_element_type=jnp.float32
        )
        summed = part_sum
        return (fresh, total, summed)

    return (absorb, init)


def finish(carry, shape):
    best, total, summed = carry
    attended = summed / jnp.transpose(total, (0, 2, 1))[..., None]
    return attended.astype(jnp.bfloat16).reshape(shape)


def identity_piece(piece):
    return piece


def per_device(
    tokens,
    conv_taps,
    norm_first,
    norm_second,
    norm_third,
    w_in,
    w_out,
    w_query,
    w_key,
    w_value,
    w_output,
    agent_order,
    present_steps,
):
    step_count, agent_count, width = tokens.shape
    reach = conv_taps.shape[0] - 1
    earlier_steps = shifted(tokens, "tm", 1)
    extended = normed_rows(jnp.concatenate([earlier_steps, tokens], axis=0), norm_first)
    mixed = jnp.zeros((step_count, agent_count, width), jnp.float32)
    for lag in range(reach + 1):
        mixed = mixed + conv_taps[lag] * extended[reach - lag : reach - lag + step_count]
    first = (tokens.astype(jnp.float32) + mixed).astype(jnp.bfloat16)
    flat = first.reshape(step_count * agent_count, width)
    inner = normed_rows(flat, norm_second).astype(jnp.bfloat16)
    hidden = jax.nn.gelu(
        jnp.dot(inner, w_in, preferred_element_type=jnp.float32), approximate=False
    ).astype(jnp.bfloat16)
    second = (
        flat.astype(jnp.float32) + jnp.dot(hidden, w_out, preferred_element_type=jnp.float32)
    ).astype(jnp.bfloat16)
    attn_in = normed_rows(second, norm_third).astype(jnp.bfloat16)
    query = (
        jnp.dot(attn_in, w_query, preferred_element_type=jnp.float32)
        .astype(jnp.bfloat16)
        .reshape(step_count, agent_count, width)
    )
    order_rows = agent_order.reshape(1, agent_count)
    present_rows = present_steps.reshape(1, agent_count)
    keys = (
        jnp.dot(attn_in, w_key, preferred_element_type=jnp.float32)
        .astype(jnp.bfloat16)
        .reshape(step_count, agent_count, width)
    )
    values = (
        jnp.dot(attn_in, w_value, preferred_element_type=jnp.float32)
        .astype(jnp.bfloat16)
        .reshape(step_count, agent_count, width)
    )
    keys, values = (keys, values)
    query, keys, values = (
        lax.all_to_all(query, "tm", split_axis=2, concat_axis=0, tiled=True),
        lax.all_to_all(keys, "tm", split_axis=2, concat_axis=0, tiled=True),
        lax.all_to_all(values, "tm", split_axis=2, concat_axis=0, tiled=True),
    )
    steps = jnp.arange(query.shape[0], dtype=jnp.int32)
    heads_here = HEADS // lax.axis_size("tm")
    absorb, init = make_absorb(query, agent_order, steps, heads_here, identity_piece)
    carry = absorb(
        init,
        (
            lax.all_gather(keys, "agent", axis=1, tiled=True),
            lax.all_gather(values, "agent", axis=1, tiled=True),
            lax.all_gather(order_rows, "agent", axis=1, tiled=True),
            lax.all_gather(present_rows, "agent", axis=1, tiled=True),
        ),
        jnp.int32(0),
    )
    attended = finish(carry, query.shape)
    attended = lax.all_to_all(attended, "tm", split_axis=0, concat_axis=2, tiled=True)
    projected = jnp.dot(
        attended.reshape(step_count * agent_count, width),
        w_output,
        preferred_element_type=jnp.float32,
    )
    result = second.astype(jnp.float32) + projected
    return result.astype(jnp.bfloat16).reshape(step_count, agent_count, width)


def solution(mesh):
    in_specs = (
        P("tm", "agent", None),
        P(),
        P(),
        P(),
        P(),
        P(),
        P(),
        P(),
        P(),
        P(),
        P(),
        P("agent"),
        P("agent"),
    )
    out_specs = P("tm", "agent", None)
    return jax.shard_map(
        per_device, mesh=mesh, in_specs=in_specs, out_specs=out_specs, check_vma=False
    )
```

profile of v0, /device:TPU:0, one launch (start us, length us, event | category | flops | bytes accessed | tf_op | source)
XLA Modules:
  0.0 235.1 jit_solution(14129081017646608805)
XLA Ops:
  6.5 5.3 %collective-permute-start = (bf16[4,64,1024]{2,1,0:T(8,128)(2,1)}, bf16[4,64,1024]{2,1,0:T(8,128)(2,1)S(1)}, u32[]{:S(2)}, u32[]{:S(2)}) collective-permute-start(bf16[4,64,1024]{2,1,0:T(8,128)(2,1)} %param.13), channel_id=1, source_target_pairs={{0,16},{16,32},{32,48},{48,64},{64,80},{80,96},{96,112},{1,17},{17... | collective-permute-start | bytes 1572872 | tf_op jit(solution)/shard_map/ppermute | solution.py:13
  11.8 1.0 fusion.102
  12.8 10.5 %collective-permute-done = bf16[4,64,1024]{2,1,0:T(8,128)(2,1)S(1)} collective-permute-done((bf16[4,64,1024]{2,1,0:T(8,128)(2,1)}, bf16[4,64,1024]{2,1,0:T(8,128)(2,1)S(1)}, u32[]{:S(2)}, u32[]{:S(2)}) %collective-permute-start) | collective-permute-done | bytes 524320 | tf_op jit(solution)/shard_map/ppermute | solution.py:13
  23.3 1.3 fusion.11
  24.6 1.3 fusion.12
  26.0 0.6 multiply_reduce_fusion
  26.6 0.1 rsqrt.29
  26.7 0.2 fusion.63
  26.9 15.0 %fusion.53 = (f32[256]{0:T(256)S(1)}, bf16[256,1024]{1,0:T(8,128)(2,1)}) fusion(bf16[3072,1024]{1,0:T(8,128)(2,1)} %param.19, bf16[256,1024]{1,0:T(8,128)(2,1)S(1)} %fusion.63, bf16[1024,3072]{1,0:T(8,128)(2,1)} %param.18, bf16[256,1024]{1,0:T(8,128)(2,1)S(1)} %bitcast.69), kind=kOutput, calls=%fused_computation.70 | convolution fusion | flops 3273916160 | bytes 14156800 | tf_op jit(solution)/shard_map/dot_general | solution.py:102
  41.9 1.8 convolution_convert_fusion
  43.8 0.9 copy.31
  44.7 0.7 reshape.197
  45.4 18.3 %all_to_all.66 = bf16[8,2,16384]{2,1,0:T(2,128)(2,1)S(1)} all-to-all(bf16[8,2,16384]{2,1,0:T(2,128)(2,1)S(1)} %reshape.197), channel_id=1, replica_groups=mesh['tm'=8,'agent'=16] {'tm'}, dimensions={0} | all-to-all | bytes 1048576 | tf_op jit(solution)/shard_map/all_to_all | solution.py:125
  63.7 0.7 reshape.198
  64.3 1.4 copy.32
  65.7 0.0 all-gather.5.cloned.1.call-start
  65.8 2.4 %convolution_convert_fusion.2 = bf16[256,1024]{1,0:T(8,128)(2,1)S(1)} fusion(bf16[1024,1024]{1,0:T(8,128)(2,1)} %param.22, bf16[256,1024]{1,0:T(8,128)(2,1)S(1)} %copy-done.8, f32[1024]{0:T(1024)S(1)} %copy-done.5, f32[256]{0:T(256)S(1)} %add_rsqrt_fusion.2), kind=kOutput, calls=%fused_computation.68 | convolution fusion | flops 538181632 | bytes 3150848 | tf_op jit(solution)/shard_map/dot_general | solution.py:118
  68.2 0.7 copy.25
  68.9 0.7 reshape.195
  69.6 17.9 %all_to_all.67 = bf16[8,2,16384]{2,1,0:T(2,128)(2,1)S(1)} all-to-all(bf16[8,2,16384]{2,1,0:T(2,128)(2,1)S(1)} %reshape.195), channel_id=1, replica_groups=mesh['tm'=8,'agent'=16] {'tm'}, dimensions={0} | all-to-all | bytes 1048576 | tf_op jit(solution)/shard_map/all_to_all | solution.py:126
  87.5 0.7 reshape.196
  88.2 1.3 copy.26
  89.5 0.0 all-gather.5.cloned.1.call-update
  89.6 0.7 dynamic-slice
  91.0 0.2 dynamic-update-slice
  91.2 0.2 dynamic-update-slice.1
  91.4 14.2 %all-reduce.2 = (s32[1024]{0:T(1024)S(1)}, s32[1024]{0:T(1024)S(1)}) all-reduce(s32[1024]{0:T(1024)S(1)} %dynamic-update-slice, s32[1024]{0:T(1024)S(1)} %dynamic-update-slice.1), channel_id=2, replica_groups=mesh['tm'=8,'agent'=16] {'agent'}, use_global_device_ids=true, to_apply=%add | all-reduce | flops 2048 | bytes 16384
  105.7 0.1 broadcast_compare_fusion.1
  105.9 2.4 %convolution_convert_fusion.1 = bf16[256,1024]{1,0:T(8,128)(2,1)S(1)} fusion(bf16[1024,1024]{1,0:T(8,128)(2,1)} %param.20, bf16[256,1024]{1,0:T(8,128)(2,1)S(1)} %copy-done.8, f32[1024]{0:T(1024)S(1)} %copy-done.5, f32[256]{0:T(256)S(1)} %add_rsqrt_fusion.2), kind=kOutput, calls=%fused_computation.67 | convolution fusion | flops 538181632 | bytes 3150848 | tf_op jit(solution)/shard_map/dot_general | solution.py:106
  108.3 0.7 copy.28
  109.0 1.5 reshape.199
  110.5 4.4 %all-to-all-start.1 = ((bf16[8,2,16384]{2,1,0:T(2,128)(2,1)}), bf16[8,2,16384]{2,1,0:T(2,128)(2,1)}, u32[]{:S(2)}, u32[]{:S(2)}) async-start(bf16[8,2,16384]{2,1,0:T(2,128)(2,1)} %reshape.199), calls=%async_computation.1 | async-start | bytes 1048576 | tf_op jit(solution)/shard_map/all_to_all | solution.py:124
  114.9 1.4 and_or_fusion
  116.3 10.8 %all-to-all-done.1 = bf16[8,2,16384]{2,1,0:T(2,128)(2,1)} async-done(((bf16[8,2,16384]{2,1,0:T(2,128)(2,1)}), bf16[8,2,16384]{2,1,0:T(2,128)(2,1)}, u32[]{:S(2)}, u32[]{:S(2)}) %all-to-all-start.1) | async-done | bytes 524320 | tf_op jit(solution)/shard_map/all_to_all | solution.py:124
  127.1 2.7 %reshape.200 = bf16[1024,4,64]{2,1,0:T(4,128)(2,1)S(1)} reshape(bf16[8,2,16384]{2,1,0:T(2,128)(2,1)} %all-to-all-done.1) | data formatting | bytes 1048576
  129.8 1.2 copy.38
  131.0 2.4 %reshape.174 = bf16[32,64,2,64]{3,2,1,0:T(2,128)(2,1)S(1)} reshape(bf16[8,4,64,128]{3,2,1,0:T(8,128)(2,1)} %bitcast.70) | data formatting | bytes 1048576 | tf_op jit(solution)/shard_map/reshape | solution.py:26
  133.5 0.0 all-gather.7.cloned.1.call-done
  133.5 12.5 %copy.33 = bf16[32,1024,128]{1,2,0:T(8,128)(2,1)} copy(bf16[32,1024,128]{2,0,1:T(8,128)(2,1)} %all-gather.7.cloned.1.call-done) | data formatting | bytes 16777216 | tf_op jit(solution)/shard_map/all_gather | solution.py:134
  146.0 10.3 %fusion = (f32[32,2,64]{2,1,0:T(2,128)S(1)}, f32[32,2,64,1024]{3,2,1,0:T(8,128)}) fusion(pred[32,64,1024]{2,1,0:T(8,128)(4,1)S(1)} %and_or_fusion, bf16[32,1024,2,64]{1,3,2,0:T(8,128)(2,1)} %bitcast.61, bf16[32,64,2,64]{3,2,1,0:T(2,128)(2,1)S(1)} %reshape.174), kind=kOutput, calls=%fused_computation.3 | convolution fusion | flops 549449728 | bytes 27803648 | tf_op jit(solution)/shard_map/sahd,sbhd->shab/dot_general | solution.py:40
  156.3 9.0 %convert_reduce_fusion = f32[32,2,64]{2,1,0:T(2,128)S(1)} fusion(f32[32,2,64]{2,1,0:T(2,128)S(1)} %broadcast_maximum_fusion, f32[32,2,64,1024]{3,2,1,0:T(8,128)} %get-tuple-element.19, pred[32,64,1024]{2,1,0:T(8,128)(4,1)S(1)} %and_or_fusion), kind=kLoop, calls=%fused_computation | loop fusion | flops 29356032 | bytes 18907136 | tf_op jit(solution)/shard_map/reduce_sum | solution.py:53
  165.3 15.4 %all-gather.5.cloned.1.call-done = bf16[32,1024,128]{2,0,1:T(8,128)(2,1)} async-done(((bf16[32,64,128]{2,0,1:T(8,128)(2,1)}), bf16[32,1024,128]{2,0,1:T(8,128)(2,1)}) %all-gather.5.cloned.1.call-update) | async-done | bytes 8388624 | tf_op jit(solution)/shard_map/all_gather | solution.py:135
  180.7 12.2 %copy.27 = bf16[32,1024,128]{1,2,0:T(8,128)(2,1)} copy(bf16[32,1024,128]{2,0,1:T(8,128)(2,1)} %all-gather.5.cloned.1.call-done) | data formatting | bytes 16777216 | tf_op jit(solution)/shard_map/all_gather | solution.py:135
  192.9 11.7 %fusion.13 = bf16[32,64,2,64]{1,3,2,0:T(8,128)(2,1)} fusion(bf16[32,1024,2,64]{1,3,2,0:T(8,128)(2,1)} %bitcast.62, f32[32,64,2]{1,2,0:T(2,128)S(1)} %bitcast.79, f32[32,2,64,1024]{3,2,1,0:T(8,128)} %get-tuple-element.19, f32[32,2,64]{2,1,0:T(2,128)S(1)} %broadcast_maximum_fusion, pred[32,64,1024]{2,1,0:T(8,128)(4,1)S(1)} %and_or_fusion), kind=kOutput, calls=%fused_computation.29 | convolution fusion | flops 558366720 | bytes 27820032 | tf_op jit(solution)/shard_map/shab,sbhd->sahd/dot_general | solution.py:54
  204.6 1.7 copy.35
  206.3 18.5 %all_to_all.68 = bf16[32,64,128]{2,1,0:T(8,128)(2,1)S(1)} all-to-all(bf16[32,64,128]{2,1,0:T(8,128)(2,1)S(1)} %copy.35), channel_id=1, replica_groups=mesh['tm'=8,'agent'=16] {'tm'}, dimensions={0} | all-to-all | bytes 1048576 | tf_op jit(solution)/shard_map/all_to_all | solution.py:142
  224.8 0.3 copy.36
  225.2 3.1 %fusion.49 = bf16[256,1024]{1,0:T(8,128)(2,1)} fusion(bf16[1024,1024]{1,0:T(8,128)(2,1)} %param.23, bf16[256,1024]{1,0:T(8,128)(2,1)S(1)} %copy-done.9, bf16[32,8,8,128]{3,2,1,0:T(8,128)(2,1)S(1)} %bitcast.78), kind=kOutput, calls=%fused_computation.65 | convolution fusion | flops 537657344 | bytes 3670016 | tf_op jit(solution)/shard_map/dot_general | solution.py:143
  (29 shorter events, 0.1 us)
Async XLA Ops:
  6.5 35.4 %copy-start = (bf16[1024,1024]{1,0:T(8,128)(2,1)S(1)}, bf16[1024,1024]{1,0:T(8,128)(2,1)}, u32[]{:S(2)}) copy-start(bf16[1024,1024]{1,0:T(8,128)(2,1)} %param.21) | copy-start | bytes 6291460
  6.5 19.4 %copy-start.2 = (bf16[4,64,1024]{2,1,0:T(8,128)(2,1)S(1)}, bf16[4,64,1024]{2,1,0:T(8,128)(2,1)}, u32[]{:S(2)}) copy-start(bf16[4,64,1024]{2,1,0:T(8,128)(2,1)} %param.13) | copy-start | bytes 1572868
  6.5 127.0 %all-gather.7.cloned.1.call-start = ((), (), s32[]{:S(2)}) async-start(), calls=%async_computation.5 | async-start | bytes 8912896 | tf_op jit(solution)/shard_map/all_gather | solution.py:134
  6.5 16.8 %collective-permute-start = (bf16[4,64,1024]{2,1,0:T(8,128)(2,1)}, bf16[4,64,1024]{2,1,0:T(8,128)(2,1)S(1)}, u32[]{:S(2)}, u32[]{:S(2)}) collective-permute-start(bf16[4,64,1024]{2,1,0:T(8,128)(2,1)} %param.13), channel_id=1, source_target_pairs={{0,16},{16,32},{32,48},{48,64},{64,80},{80,96},{96,112},{1,17},{17... | collective-permute-start | bytes 1572872 | tf_op jit(solution)/shard_map/ppermute | solution.py:13
  26.0 0.7 copy-start.3
  26.9 15.1 %copy-start.5 = (f32[1024]{0:T(1024)S(1)}, f32[1024]{0:T(1024)}, u32[]{:S(2)}) copy-start(f32[1024]{0:T(1024)} %param.17) | copy-start | bytes 12292
  44.6 21.1 %copy-start.8 = (bf16[256,1024]{1,0:T(8,128)(2,1)S(1)}, bf16[256,1024]{1,0:T(8,128)(2,1)}, u32[]{:S(2)}) copy-start(bf16[256,1024]{1,0:T(8,128)(2,1)} %get-tuple-element.17) | copy-start | bytes 1572868
  65.7 114.9 %all-gather.5.cloned.1.call-start = ((), (), s32[]{:S(2)}) async-start(), calls=%async_computation.4 | async-start | bytes 8912896 | tf_op jit(solution)/shard_map/all_gather | solution.py:135
  68.9 20.7 %copy-start.7 = (u32[128]{0:T(128)S(1)}, u32[128]{0:T(128)}, u32[]{:S(2)}) copy-start(u32[128]{0:T(128)} %constant.80) | copy-start | bytes 1540
  68.9 22.1 %copy-start.4 = (s32[64]{0:T(128)S(1)}, s32[64]{0:T(128)}, u32[]{:S(2)}) copy-start(s32[64]{0:T(128)} %param.24) | copy-start | bytes 772
  68.9 22.3 %copy-start.6 = (s32[64]{0:T(128)S(1)}, s32[64]{0:T(128)}, u32[]{:S(2)}) copy-start(s32[64]{0:T(128)} %param.25) | copy-start | bytes 772
  110.5 16.5 %all-to-all-start.1 = ((bf16[8,2,16384]{2,1,0:T(2,128)(2,1)}), bf16[8,2,16384]{2,1,0:T(2,128)(2,1)}, u32[]{:S(2)}, u32[]{:S(2)}) async-start(bf16[8,2,16384]{2,1,0:T(2,128)(2,1)} %reshape.199), calls=%async_computation.1 | async-start | bytes 1048576 | tf_op jit(solution)/shard_map/all_to_all | solution.py:124
  204.6 20.6 %copy-start.9 = (bf16[256,1024]{1,0:T(8,128)(2,1)S(1)}, bf16[256,1024]{1,0:T(8,128)(2,1)}, u32[]{:S(2)}) copy-start(bf16[256,1024]{1,0:T(8,128)(2,1)} %get-tuple-element.17) | copy-start | bytes 1572868
  204.6 23.7 %copy-start.1 = (bf16[1024,1024]{1,0:T(8,128)(2,1)S(1)}, bf16[1024,1024]{1,0:T(8,128)(2,1)}, u32[]{:S(2)}) copy-start(bf16[1024,1024]{1,0:T(8,128)(2,1)} %param.21) | copy-start | bytes 6291460
Sparse Core Ops, SparseCore 0:
  65.8 53.2 all-gather.6
  120.8 59.7 all-gather.4
where the time goes:
time: 236 us; the launch traced here: 235 us
  blocking collectives  69 us (29%)
  matrix products  46.8 us (20%)
  local copies, waits for them, and re-layouts  44.6 us (19%)
  waiting for transfers between devices  36.7 us (16%)
  between operations  14.4 us (6%)
  other arithmetic  14 us (6%)
  starting transfers between devices  9.7 us (4%)
    all_to_all x1, blocking collectives, per_device(): lax.all_to_all(attended, 'tm', split_axis=0, concat_axis=2, tiled=True)  18.5 us
    all_to_all x1, blocking collectives, per_device(): lax.all_to_all(keys, 'tm', split_axis=2, concat_axis=0, tiled=True)  18.3 us
    all_to_all x1, blocking collectives, per_device(): lax.all_to_all(values, 'tm', split_axis=2, concat_axis=0, tiled=True)  17.9 us
    all_gather x1, waiting for transfers between devices, per_device(): lax.all_gather(values, 'agent', axis=1, tiled=True)  15.4 us
    dot_general x1, matrix products, per_device(): jnp.dot(hidden, w_out, preferred_element_type=jnp.float32)  15 us
    unnamed x1, blocking collectives  14.2 us
    all_gather x1, local copies, waits for them, and re-layouts, per_device(): lax.all_gather(keys, 'agent', axis=1, tiled=True)  12.5 us
    all_gather x1, local copies, waits for them, and re-layouts, per_device(): lax.all_gather(values, 'agent', axis=1, tiled=True)  12.2 us
  transfers between devices with their start and end apart: 4, of which 3 were waited for; matrix products, arithmetic and copies ran while one was open for 22% of the time, Pallas kernels for 0%

commit v1 on v0

--- a/solution.py
+++ b/solution.py
@@ -131,7 +131,9 @@
     carry = absorb(
         init,
         (
-            lax.all_gather(keys, "agent", axis=1, tiled=True),
+            jnp.concatenate(
+                lax.all_to_all(jnp.stack([keys] * lax.axis_size("agent")), "agent", 0, 0), axis=1
+            ),
             lax.all_gather(values, "agent", axis=1, tiled=True),
             lax.all_gather(order_rows, "agent", axis=1, tiled=True),
             lax.all_gather(present_rows, "agent", axis=1, tiled=True),

time: 236 us -> 353 us (1.50)
  blocking collectives: 69 us -> 139 us
  local copies, waits for them, and re-layouts: 44.6 us -> 79 us
  starting transfers between devices: 9.7 us -> 19.2 us
    unnamed x1, blocking collectives: 14.2 us -> 99.1 us
    another operation x0 -> x2, local copies, waits for them, and re-layouts: none -> 28 us  [the longest x1 22.6 us: absorb(): key_piece = key_piece.reshape(step_count, count, heads_here, head_size)]
    reshape x0 -> x1, local copies, waits for them, and re-layouts: none -> 18.7 us  [per_device(): jnp.concatenate(lax.all_to_all(jnp.stack([keys] * lax.axis_size('agent'))...]
    all_to_all x1 -> x0, blocking collectives: 18.3 us -> none  [per_device(): lax.all_to_all(keys, 'tm', split_axis=2, concat_axis=0, tiled=True)]
    all_gather x1, waiting for transfers between devices: 15.4 us -> 0.02 us  [per_device(): lax.all_gather(values, 'agent', axis=1, tiled=True)]
    all_gather x1 -> x0, local copies, waits for them, and re-layouts: 12.5 us -> none  [per_device(): lax.all_gather(keys, 'agent', axis=1, tiled=True)]
    all_to_all x0 -> x2, waiting for transfers between devices: none -> 12 us  [the longest x1 12 us: per_device(): lax.all_to_all(keys, 'tm', split_axis=2, concat_axis=0, tiled=True)]
    all_to_all x0 -> x2, starting transfers between devices: none -> 10.4 us  [the longest x1 6.88 us: per_device(): lax.all_to_all(jnp.stack([keys] * lax.axis_size('agent')), 'agent', 0, 0)]
  transfers between devices with their start and end apart: 4 -> 5, of which waited for: 3 -> 3; matrix products, arithmetic and copies ran while one was open for 22% -> 25% of each run, Pallas kernels for 0% -> 0%
where the time goes in v1:
time: 353 us; the launch traced here: 349 us
  blocking collectives  139 us (39%)
  local copies, waits for them, and re-layouts  79 us (22%)
  matrix products  46.4 us (13%)
  waiting for transfers between devices  37.7 us (11%)
  starting transfers between devices  19.2 us (5%)
  between operations  14.3 us (4%)
  other arithmetic  13.9 us (4%)
    unnamed x1, blocking collectives  99.1 us
    another operation x1, local copies, waits for them, and re-layouts, absorb(): key_piece = key_piece.reshape(step_count, count, heads_here, head_size)  22.6 us
    all_to_all x1, blocking collectives, per_device(): lax.all_to_all(attended, 'tm', split_axis=0, concat_axis=2, tiled=True)  21.5 us
    reshape x1, local copies, waits for them, and re-layouts, per_device(): jnp.concatenate(lax.all_to_all(jnp.stack([keys] * lax.axis_size('agent'))...  18.7 us
    all_to_all x1, blocking collectives, per_device(): lax.all_to_all(values, 'tm', split_axis=2, concat_axis=0, tiled=True)  18.3 us
    all_to_all x1, waiting for transfers between devices, per_device(): lax.all_to_all(query, 'tm', split_axis=2, concat_axis=0, tiled=True)  15.1 us
    dot_general x1, matrix products, per_device(): jnp.dot(hidden, w_out, preferred_element_type=jnp.float32)  15 us
    all_gather x1, local copies, waits for them, and re-layouts, per_device(): lax.all_gather(values, 'agent', axis=1, tiled=True)  12.2 us
  transfers between devices with their start and end apart: 5, of which 3 were waited for; matrix products, arithmetic and copies ran while one was open for 25% of the time, Pallas kernels for 0%

profile of v1, /device:TPU:0, one launch (start us, length us, event | category | flops | bytes accessed | tf_op | source)
XLA Modules:
  0.0 349.4 jit_solution(12880504687697954196)
XLA Ops:
  6.5 5.3 %collective-permute-start = (bf16[4,64,1024]{2,1,0:T(8,128)(2,1)}, bf16[4,64,1024]{2,1,0:T(8,128)(2,1)S(1)}, u32[]{:S(2)}, u32[]{:S(2)}) collective-permute-start(bf16[4,64,1024]{2,1,0:T(8,128)(2,1)} %param.13), channel_id=1, source_target_pairs={{0,16},{16,32},{32,48},{48,64},{64,80},{80,96},{96,112},{1,17},{17... | collective-permute-start | bytes 1572872 | tf_op jit(solution)/shard_map/ppermute | solution.py:13
  11.8 1.0 fusion.102
  12.8 10.5 %collective-permute-done = bf16[4,64,1024]{2,1,0:T(8,128)(2,1)S(1)} collective-permute-done((bf16[4,64,1024]{2,1,0:T(8,128)(2,1)}, bf16[4,64,1024]{2,1,0:T(8,128)(2,1)S(1)}, u32[]{:S(2)}, u32[]{:S(2)}) %collective-permute-start) | collective-permute-done | bytes 524320 | tf_op jit(solution)/shard_map/ppermute | solution.py:13
  23.3 1.3 fusion.11
  24.6 1.3 fusion.12
  26.0 0.6 multiply_reduce_fusion
  26.6 0.1 rsqrt.29
  26.7 0.2 fusion.63
  26.9 15.0 %fusion.53 = (f32[256]{0:T(256)S(1)}, bf16[256,1024]{1,0:T(8,128)(2,1)}) fusion(bf16[3072,1024]{1,0:T(8,128)(2,1)} %param.19, bf16[256,1024]{1,0:T(8,128)(2,1)S(1)} %fusion.63, bf16[1024,3072]{1,0:T(8,128)(2,1)} %param.18, bf16[256,1024]{1,0:T(8,128)(2,1)S(1)} %bitcast.73), kind=kOutput, calls=%fused_computation.70 | convolution fusion | flops 3273916160 | bytes 14156800 | tf_op jit(solution)/shard_map/dot_general | solution.py:102
  41.9 1.8 convolution_convert_fusion.2
  43.8 0.9 copy.25
  44.7 0.7 reshape.198
  45.4 18.3 %all_to_all.68 = bf16[8,2,16384]{2,1,0:T(2,128)(2,1)S(1)} all-to-all(bf16[8,2,16384]{2,1,0:T(2,128)(2,1)S(1)} %reshape.198), channel_id=1, replica_groups=mesh['tm'=8,'agent'=16] {'tm'}, dimensions={0} | all-to-all | bytes 1048576 | tf_op jit(solution)/shard_map/all_to_all | solution.py:126
  63.7 0.7 reshape.199
  64.3 1.3 copy.26
  65.7 2.4 convolution_convert_fusion
  68.1 0.7 copy.31
  68.8 1.5 reshape.200
  70.3 3.5 all-to-all-start.2
  73.8 2.3 convolution_convert_fusion.1
  76.2 0.7 copy.28
  76.9 1.5 reshape.202
  78.5 12.0 %all-to-all-done.2 = bf16[8,2,16384]{2,1,0:T(2,128)(2,1)S(1)} async-done(((bf16[8,2,16384]{2,1,0:T(2,128)(2,1)}), bf16[8,2,16384]{2,1,0:T(2,128)(2,1)S(1)}, u32[]{:S(2)}, u32[]{:S(2)}) %all-to-all-start.2) | async-done | bytes 524320 | tf_op jit(solution)/shard_map/all_to_all | solution.py:125
  90.5 3.5 %all-to-all-start.1 = ((bf16[8,2,16384]{2,1,0:T(2,128)(2,1)}), bf16[8,2,16384]{2,1,0:T(2,128)(2,1)S(1)}, u32[]{:S(2)}, u32[]{:S(2)}) async-start(bf16[8,2,16384]{2,1,0:T(2,128)(2,1)} %reshape.202), calls=%async_computation.1 | async-start | bytes 1048576 | tf_op jit(solution)/shard_map/all_to_all | solution.py:124
  94.0 0.7 reshape.201
  94.6 0.6 copy.41
  95.2 15.1 %all-to-all-done.1 = bf16[8,2,16384]{2,1,0:T(2,128)(2,1)S(1)} async-done(((bf16[8,2,16384]{2,1,0:T(2,128)(2,1)}), bf16[8,2,16384]{2,1,0:T(2,128)(2,1)S(1)}, u32[]{:S(2)}, u32[]{:S(2)}) %all-to-all-start.1) | async-done | bytes 524320 | tf_op jit(solution)/shard_map/all_to_all | solution.py:124
  110.3 5.4 %stack.5 = bf16[16,32,64,128]{3,2,1,0:T(8,128)(2,1)} broadcast(bf16[32,64,128]{2,1,0:T(8,128)(2,1)S(1)} %bitcast.74), dimensions={1,2,3} | broadcast | bytes 8912896 | tf_op jit(solution)/shard_map/stack | solution.py:135
  115.7 6.9 %all-to-all-start.3 = ((bf16[16,32,64,128]{3,2,1,0:T(8,128)(2,1)}), bf16[16,32,64,128]{3,2,1,0:T(8,128)(2,1)}, u32[]{:S(2)}, u32[]{:S(2)}) async-start(bf16[16,32,64,128]{3,2,1,0:T(8,128)(2,1)} %stack.5), calls=%async_computation.3 | async-start | bytes 16777216 | tf_op jit(solution)/shard_map/all_to_all | solution.py:135
  122.6 0.6 dynamic-slice
  123.8 0.2 dynamic-update-slice
  124.0 0.2 dynamic-update-slice.1
  124.2 99.1 %all-reduce.2 = (s32[1024]{0:T(1024)S(1)}, s32[1024]{0:T(1024)S(1)}) all-reduce(s32[1024]{0:T(1024)S(1)} %dynamic-update-slice, s32[1024]{0:T(1024)S(1)} %dynamic-update-slice.1), channel_id=2, replica_groups=mesh['tm'=8,'agent'=16] {'agent'}, use_global_device_ids=true, to_apply=%add | all-reduce | flops 2048 | bytes 16384
  223.4 0.1 broadcast_compare_fusion.1
  223.5 1.4 and_or_fusion
  224.9 3.0 reshape.203
  227.9 1.2 copy.39
  229.1 2.4 reshape.177
  231.6 18.7 %copy.34 = bf16[32,16,64,128]{2,1,3,0:T(8,128)(2,1)} copy(bf16[32,16,64,128]{3,2,0,1:T(8,128)(2,1)} %bitcast.21) | data formatting | bytes 16777216 | tf_op jit(solution)/shard_map/reshape | solution.py:134
  250.3 22.6 %reshape_reshape.3 = bf16[32,1024,2,64]{1,3,2,0:T(8,128)(2,1)} reshape(bf16[32,16,64,128]{2,1,3,0:T(8,128)(2,1)} %copy.34) | data formatting | bytes 16777216 | tf_op jit(solution)/shard_map/reshape;reshape | solution.py:37
  272.9 10.1 %fusion = (f32[32,2,64]{2,1,0:T(2,128)S(1)}, f32[32,2,64,1024]{3,2,1,0:T(8,128)}) fusion(pred[32,64,1024]{2,1,0:T(8,128)(4,1)S(1)} %and_or_fusion, bf16[32,1024,2,64]{1,3,2,0:T(8,128)(2,1)} %reshape_reshape.3, bf16[32,64,2,64]{3,2,1,0:T(2,128)(2,1)S(1)} %reshape.177), kind=kOutput, calls=%fused_computation.3 | convolution fusion | flops 549449728 | bytes 27803648 | tf_op jit(solution)/shard_map/sahd,sbhd->shab/dot_general | solution.py:40
  283.0 8.8 %convert_reduce_fusion = f32[32,2,64]{2,1,0:T(2,128)S(1)} fusion(f32[32,2,64]{2,1,0:T(2,128)S(1)} %broadcast_maximum_fusion, f32[32,2,64,1024]{3,2,1,0:T(8,128)} %get-tuple-element.19, pred[32,64,1024]{2,1,0:T(8,128)(4,1)S(1)} %and_or_fusion), kind=kLoop, calls=%fused_computation | loop fusion | flops 29356032 | bytes 18907136 | tf_op jit(solution)/shard_map/reduce_sum | solution.py:53
  291.8 12.2 %copy.27 = bf16[32,1024,128]{1,2,0:T(8,128)(2,1)} copy(bf16[32,1024,128]{2,0,1:T(8,128)(2,1)} %all-gather.4.cloned.1.call-done) | data formatting | bytes 16777216 | tf_op jit(solution)/shard_map/all_gather | solution.py:137
  304.1 11.7 %fusion.13 = bf16[32,64,2,64]{1,3,2,0:T(8,128)(2,1)} fusion(bf16[32,1024,2,64]{1,3,2,0:T(8,128)(2,1)} %bitcast.66, f32[32,64,2]{1,2,0:T(2,128)S(1)} %bitcast.83, f32[32,2,64,1024]{3,2,1,0:T(8,128)} %get-tuple-element.19, f32[32,2,64]{2,1,0:T(2,128)S(1)} %broadcast_maximum_fusion, pred[32,64,1024]{2,1,0:T(8,128)(4,1)S(1)} %and_or_fusion), kind=kOutput, calls=%fused_computation.29 | convolution fusion | flops 558366720 | bytes 27820032 | tf_op jit(solution)/shard_map/shab,sbhd->sahd/dot_general | solution.py:54
  315.8 1.7 copy.36
  317.5 21.5 %all_to_all.69 = bf16[32,64,128]{2,1,0:T(8,128)(2,1)S(1)} all-to-all(bf16[32,64,128]{2,1,0:T(8,128)(2,1)S(1)} %copy.36), channel_id=1, replica_groups=mesh['tm'=8,'agent'=16] {'tm'}, dimensions={0} | all-to-all | bytes 1048576 | tf_op jit(solution)/shard_map/all_to_all | solution.py:144
  339.1 0.3 copy.37
  339.4 3.1 fusion.49
  (33 shorter events, 0.2 us)
Async XLA Ops:
  6.5 35.4 %copy-start = (bf16[1024,1024]{1,0:T(8,128)(2,1)S(1)}, bf16[1024,1024]{1,0:T(8,128)(2,1)}, u32[]{:S(2)}) copy-start(bf16[1024,1024]{1,0:T(8,128)(2,1)} %param.22) | copy-start | bytes 6291460
  6.5 19.4 %copy-start.2 = (bf16[4,64,1024]{2,1,0:T(8,128)(2,1)S(1)}, bf16[4,64,1024]{2,1,0:T(8,128)(2,1)}, u32[]{:S(2)}) copy-start(bf16[4,64,1024]{2,1,0:T(8,128)(2,1)} %param.13) | copy-start | bytes 1572868
  6.5 285.3 %all-gather.4.cloned.1.call-start = ((), (), s32[]{:S(2)}) async-start(), calls=%async_computation.5 | async-start | bytes 8912896 | tf_op jit(solution)/shard_map/all_gather | solution.py:137
  6.5 16.8 %collective-permute-start = (bf16[4,64,1024]{2,1,0:T(8,128)(2,1)}, bf16[4,64,1024]{2,1,0:T(8,128)(2,1)S(1)}, u32[]{:S(2)}, u32[]{:S(2)}) collective-permute-start(bf16[4,64,1024]{2,1,0:T(8,128)(2,1)} %param.13), channel_id=1, source_target_pairs={{0,16},{16,32},{32,48},{48,64},{64,80},{80,96},{96,112},{1,17},{17... | collective-permute-start | bytes 1572872 | tf_op jit(solution)/shard_map/ppermute | solution.py:13
  26.0 0.7 copy-start.4
  26.9 15.1 %copy-start.6 = (f32[1024]{0:T(1024)S(1)}, f32[1024]{0:T(1024)}, u32[]{:S(2)}) copy-start(f32[1024]{0:T(1024)} %param.17) | copy-start | bytes 12292
  44.6 21.1 %copy-start.9 = (bf16[256,1024]{1,0:T(8,128)(2,1)S(1)}, bf16[256,1024]{1,0:T(8,128)(2,1)}, u32[]{:S(2)}) copy-start(bf16[256,1024]{1,0:T(8,128)(2,1)} %get-tuple-element.17) | copy-start | bytes 1572868
  70.3 20.1 %all-to-all-start.2 = ((bf16[8,2,16384]{2,1,0:T(2,128)(2,1)}), bf16[8,2,16384]{2,1,0:T(2,128)(2,1)S(1)}, u32[]{:S(2)}, u32[]{:S(2)}) async-start(bf16[8,2,16384]{2,1,0:T(2,128)(2,1)} %reshape.200), calls=%async_computation.2 | async-start | bytes 1048576 | tf_op jit(solution)/shard_map/all_to_all | solution.py:125
  90.5 19.9 %all-to-all-start.1 = ((bf16[8,2,16384]{2,1,0:T(2,128)(2,1)}), bf16[8,2,16384]{2,1,0:T(2,128)(2,1)S(1)}, u32[]{:S(2)}, u32[]{:S(2)}) async-start(bf16[8,2,16384]{2,1,0:T(2,128)(2,1)} %reshape.202), calls=%async_computation.1 | async-start | bytes 1048576 | tf_op jit(solution)/shard_map/all_to_all | solution.py:124
  110.3 5.4 %copy-start.3 = (bf16[8,2,16384]{2,1,0:T(2,128)(2,1)}, bf16[8,2,16384]{2,1,0:T(2,128)(2,1)S(1)}, u32[]{:S(2)}) copy-start(bf16[8,2,16384]{2,1,0:T(2,128)(2,1)S(1)} %all-to-all-done.1) | copy-start | bytes 1572868
  115.7 6.9 %copy-start.8 = (u32[128]{0:T(128)S(1)}, u32[128]{0:T(128)}, u32[]{:S(2)}) copy-start(u32[128]{0:T(128)} %constant.80) | copy-start | bytes 1540
  115.7 8.0 %copy-start.5 = (s32[64]{0:T(128)S(1)}, s32[64]{0:T(128)}, u32[]{:S(2)}) copy-start(s32[64]{0:T(128)} %param.24) | copy-start | bytes 772
  115.7 8.3 %copy-start.7 = (s32[64]{0:T(128)S(1)}, s32[64]{0:T(128)}, u32[]{:S(2)}) copy-start(s32[64]{0:T(128)} %param.25) | copy-start | bytes 772
  115.7 115.9 %all-to-all-start.3 = ((bf16[16,32,64,128]{3,2,1,0:T(8,128)(2,1)}), bf16[16,32,64,128]{3,2,1,0:T(8,128)(2,1)}, u32[]{:S(2)}, u32[]{:S(2)}) async-start(bf16[16,32,64,128]{3,2,1,0:T(8,128)(2,1)} %stack.5), calls=%async_computation.3 | async-start | bytes 16777216 | tf_op jit(solution)/shard_map/all_to_all | solution.py:135
  315.8 23.6 %copy-start.10 = (bf16[256,1024]{1,0:T(8,128)(2,1)S(1)}, bf16[256,1024]{1,0:T(8,128)(2,1)}, u32[]{:S(2)}) copy-start(bf16[256,1024]{1,0:T(8,128)(2,1)} %get-tuple-element.17) | copy-start | bytes 1572868
  315.8 26.7 %copy-start.1 = (bf16[1024,1024]{1,0:T(8,128)(2,1)S(1)}, bf16[1024,1024]{1,0:T(8,128)(2,1)}, u32[]{:S(2)}) copy-start(bf16[1024,1024]{1,0:T(8,128)(2,1)} %param.22) | copy-start | bytes 6291460
Sparse Core Ops, SparseCore 0:
  65.8 59.2 all-gather.3
